TPU v7x, 256 devices: a whole 4x4x8 slice. The times are simulated.
256 devices in a mesh: ex: 16 (over y_hi, x, core), co: 16 (over y_lo, z).
Axes of the slice: x: 4, y: 4 (y_hi: 2, y_lo: 2; y = y_hi * 2 + y_lo), z: 8, core: 2. Of those that a mesh axis runs over, the one named last changes fastest.
Arguments:
- train_grads: float32 [16384, 32768], P('ex', 'co')
- queries: float32 [1024, 32768], P('ex', 'co'), may hold values from -6 to 6
- module_ids: int32 [8], replicated, may hold values from 0 to 223
- module_scale: float32 [224], replicated, may hold values from 0.3 to 3
- example_ids: int32 [16384], P('ex'), may hold values from 0 to 16383, as said below
Outputs:
- influence: float32 [1024, 16384], P('co', 'ex')
Inputs may be any that keep to these rules, and one draw needn't show every extreme that they name: `example_ids`: the examples of block s of 1024 rows carry the ids s * 1024 to (s + 1) * 1024 - 1, each once.
All inputs are finite; a program needn't handle non-finite values.
Results may differ from a plain program's by a relative error of at most 0.00008.
Values sent between devices are 32-bit elements; how exact they have to be, the bound alone decides.
No kernel may reach another device: no remote copies, remote signals or barrier semaphores. Data moves between devices by JAX's collectives and lax.ppermute only.
A program may use at most 128 MiB of HBM per device.

v0:
```python
import jax
import jax.numpy as jnp
from jax import lax
from jax.sharding import PartitionSpec as P

PROJ = 4096
epsilon = 1e-06


def total_of_pieces(x, axis):
    return lax.all_gather(x, axis).sum(0)


def score_block(query_rows, train_grads):
    return lax.dot_general(
        query_rows,
        train_grads,
        (((1,), (1,)), ((), ())),
        precision=lax.Precision.HIGHEST,
        preferred_element_type=jnp.float32,
    )


def shards(train_grads, queries, module_ids, module_scale, example_ids):
    example_count = train_grads.shape[0]
    coord_count = train_grads.shape[1]
    module_count = module_ids.shape[0]
    offset = lax.axis_index("co") * coord_count
    position = offset + lax.iota(jnp.int32, coord_count)
    table_index = lax.iota(jnp.int32, module_scale.shape[0])
    picked = jnp.sum(
        jnp.where(module_ids[:, None] == table_index[None, :], module_scale[None, :], 0.0), axis=1
    )
    window_index = lax.iota(jnp.int32, module_count)
    local_module = position // PROJ
    coord_scale = jnp.sum(
        jnp.where(local_module[:, None] == window_index[None, :], picked[None, :], 0.0), axis=1
    )
    scaled = queries * coord_scale[None, :]
    squares = jnp.sum(train_grads * train_grads, axis=1)
    norm_total = total_of_pieces(squares, "co")
    inverse_norm = lax.rsqrt(norm_total + epsilon)
    all_queries = lax.all_gather(scaled, "ex", axis=0, tiled=True)
    own_scores = lax.psum_scatter(
        score_block(all_queries, train_grads), "co", scatter_dimension=0, tiled=True
    )
    normed = own_scores * inverse_norm[None, :]
    local_ids = example_ids - lax.axis_index("ex") * example_count
    return jnp.zeros_like(normed).at[:, local_ids].set(normed)


def solution(mesh):
    return jax.shard_map(
        shards,
        mesh=mesh,
        in_specs=(P("ex", "co"), P("ex", "co"), P(), P(), P("ex")),
        out_specs=P("co", "ex"),
        check_vma=False,
    )
```

profile of v0, /device:TPU:2, one launch (start us, length us, event | category | flops | bytes accessed | tf_op | source)
XLA Modules:
  0.0 214.1 jit_solution(3390543927937948465)
XLA Ops:
  6.5 0.0 all-gather.3.cloned.1.call-start
  6.6 0.9 select_reduce_fusion.1
  7.4 0.1 select_reduce_fusion
  7.5 1.9 broadcast_multiply_fusion
  9.4 0.0 all-gather.3.cloned.1.call-update
  9.5 0.0 reduce-scatter.2.cloned.1.call-start
  9.5 80.2 %all-gather.3.cloned.1.call-done = f32[1024,2048]{1,0:T(8,128)} async-done(((f32[64,2048]{1,0:T(8,128)}), f32[1024,2048]{1,0:T(8,128)}) %all-gather.3.cloned.1.call-update) | async-done | bytes 8388624 | tf_op jit(solution)/shard_map/all_gather | solution.py:43
  89.7 32.1 %fusion.5 = f32[1024,1024]{1,0:T(8,128)} fusion(f32[1024,2048]{1,0:T(8,128)} %all-gather.3.cloned.1.call-done, f32[1024,2048]{1,0:T(8,128)} %param.5), kind=kOutput, calls=%fused_computation.21 | convolution fusion | flops 25769803776 | bytes 20971520 | tf_op jit(solution)/shard_map/dot_general | solution.py:15
  121.8 0.0 copy-start
  121.8 0.0 reduce-scatter.2.cloned.1.call-update
  121.8 4.0 %multiply_reduce_fusion = f32[1024]{0:T(1024)S(1)} fusion(f32[1024,2048]{1,0:T(8,128)} %param.5), kind=kLoop, calls=%fused_computation.1 | loop fusion | flops 4193280 | bytes 8392704 | tf_op jit(solution)/shard_map/reduce_sum | solution.py:40
  125.8 33.2 %all-gather = f32[16384]{0:T(1024)S(1)} all-gather(f32[1024]{0:T(1024)S(1)} %multiply_reduce_fusion), channel_id=2, replica_groups=mesh['ex'=16,'co'=16] {'co'}, dimensions={0}, use_global_device_ids=true | all-gather | bytes 69632 | tf_op jit(solution)/shard_map/all_gather | solution.py:11
  159.1 0.0 copy-done
  159.1 42.9 %reduce-scatter.2.cloned.1.call-done = f32[64,1024]{1,0:T(8,128)} async-done(((f32[1024,1024]{1,0:T(8,128)}), f32[64,1024]{1,0:T(8,128)}) %reduce-scatter.2.cloned.1.call-update) | async-done | bytes 262160 | tf_op jit(solution)/shard_map/reduce_scatter | solution.py:44
  202.0 1.0 multiply_bitcast_fusion
  203.0 0.2 copy.10
  203.2 3.2 %scatter_custom_fusion = f32[64,1024]{0,1:T(8,128)S(1)} fusion(s32[1024]{0:T(1024)S(1)} %compare_select_fusion, f32[1024,64]{1,0:T(8,128)S(1)} %copy.10, f32[]{:T(128)} %constant.11.clone.1), kind=kCustom, calls=%fused_computation.4 | custom fusion | bytes 262148 | tf_op jit(solution)/shard_map/scatter | solution.py:49
  206.4 0.9 copy.11
  (5 shorter events, 0.1 us)
Async XLA Ops:
  6.5 83.1 %all-gather.3.cloned.1.call-start = ((), (), s32[]{:S(2)}) async-start(), calls=%async_computation.1 | async-start | bytes 8912896 | tf_op jit(solution)/shard_map/all_gather | solution.py:43
  9.5 192.5 %reduce-scatter.2.cloned.1.call-start = ((), (), s32[]{:S(2)}) async-start(), calls=%async_computation.2 | async-start | bytes 4456448 | tf_op jit(solution)/shard_map/reduce_scatter | solution.py:44
  121.8 37.3 %copy-start = (s32[1024]{0:T(1024)S(1)}, s32[1024]{0:T(1024)}, u32[]{:S(2)}) copy-start(s32[1024]{0:T(1024)} %param.9) | copy-start | bytes 12292
Sparse Core Ops, SparseCore 0:
  10.1 79.5 all-gather.2
  121.9 80.0 reduce-scatter.1
where the time goes:
time: 214 us
  waiting for transfers between devices  123 us (57%)
  blocking collectives  33.2 us (16%)
  matrix products  32.1 us (15%)
  between operations  13.5 us (6%)
  other arithmetic  7.89 us (4%)
  local copies, waits for them, and re-layouts  4.32 us (2%)
    all_gather x1, waiting for transfers between devices, shards(): all_queries = lax.all_gather(scaled, 'ex', axis=0, tiled=True)  80.2 us
    reduce_scatter x1, waiting for transfers between devices, shards(): lax.psum_scatter(score_block(all_queries, train_grads), 'co', scatter_dim...  42.9 us
    all_gather x1, blocking collectives, total_of_pieces(): return lax.all_gather(x, axis).sum(0)  33.2 us
    dot_general x1, matrix products, score_block(): lax.dot_general(query_rows, train_grads, (((1,), (1,)), ((), ())), precis...  32.1 us
  transfers between devices with their start and end apart: 2, of which 2 were waited for; matrix products, arithmetic and copies ran while one was open for 2% of the time, Pallas kernels for 0%

commit v1 on v0

--- a/solution.py
+++ b/solution.py
@@ -40,7 +40,8 @@
     squares = jnp.sum(train_grads * train_grads, axis=1)
     norm_total = total_of_pieces(squares, "co")
     inverse_norm = lax.rsqrt(norm_total + epsilon)
-    all_queries = lax.all_gather(scaled, "ex", axis=0, tiled=True)
+    sent = jnp.stack([scaled] * lax.axis_size("ex"))
+    all_queries = jnp.concatenate(lax.all_to_all(sent, "ex", 0, 0), axis=0)
     own_scores = lax.psum_scatter(
         score_block(all_queries, train_grads), "co", scatter_dimension=0, tiled=True
     )

time: 214 us -> 233 us (1.089)
  blocking collectives: 33.2 us -> 136 us
  waiting for transfers between devices: 123 us -> 42.4 us
  matrix products: 32.1 us -> 27.7 us
    all_to_all x0 -> x1, blocking collectives: none -> 101 us  [shards(): all_queries = jnp.concatenate(lax.all_to_all(sent, 'ex', 0, 0), axis=0)]
    all_gather x1 -> x0, waiting for transfers between devices: 80.2 us -> none  [shards(): all_queries = lax.all_gather(scaled, 'ex', axis=0, tiled=True)]
    dot_general x1, matrix products: 32.1 us -> 27.7 us  [score_block(): lax.dot_general(query_rows, train_grads, (((1,), (1,)), ((), ())), precis...]
    all_gather x1, blocking collectives: 33.2 us -> 35.9 us  [total_of_pieces(): return lax.all_gather(x, axis).sum(0)]
  transfers between devices with their start and end apart: 2 -> 1, of which waited for: 2 -> 1; matrix products, arithmetic and copies ran while one was open for 2% -> 2% of each run, Pallas kernels for 0% -> 0%
where the time goes in v1:
time: 233 us; the launch traced here: 232 us
  blocking collectives  136 us (58%)
  waiting for transfers between devices  42.4 us (18%)
  matrix products  27.7 us (12%)
  between operations  13.5 us (6%)
  other arithmetic  7.05 us (3%)
  local copies, waits for them, and re-layouts  5.4 us (2%)
    all_to_all x1, blocking collectives, shards(): all_queries = jnp.concatenate(lax.all_to_all(sent, 'ex', 0, 0), axis=0)  101 us
    reduce_scatter x1, waiting for transfers between devices, shards(): lax.psum_scatter(score_block(all_queries, train_grads), 'co', scatter_dim...  42.4 us
    all_gather x1, blocking collectives, total_of_pieces(): return lax.all_gather(x, axis).sum(0)  35.9 us
    dot_general x1, matrix products, score_block(): lax.dot_general(query_rows, train_grads, (((1,), (1,)), ((), ())), precis...  27.7 us
  transfers between devices with their start and end apart: 1, of which 1 were waited for; matrix products, arithmetic and copies ran while one was open for 2% of the time, Pallas kernels for 0%

profile of v1, /device:TPU:2, one launch (start us, length us, event | category | flops | bytes accessed | tf_op | source)
XLA Modules:
  0.0 232.5 jit_solution(7067178665674551717)
XLA Ops:
  6.5 0.0 reduce-scatter.2.cloned.1.call-start
  6.6 0.9 select_reduce_fusion.1
  7.4 0.1 select_reduce_fusion
  7.5 1.1 broadcast_multiply_fusion
  8.6 0.0 slice-start
  8.6 1.1 stack.2
  9.7 0.0 slice-start.1
  9.7 100.5 %all_to_all.5 = f32[16,64,2048]{2,1,0:T(8,128)S(1)} all-to-all(f32[16,64,2048]{2,1,0:T(8,128)S(1)} %stack.2), channel_id=1, replica_groups=mesh['ex'=16,'co'=16] {'ex'}, dimensions={0} | all-to-all | bytes 16777216 | tf_op jit(solution)/shard_map/all_to_all | solution.py:44
  110.2 0.0 slice-done
  110.2 0.0 slice-done.1
  110.2 27.7 %fusion.5 = f32[1024,1024]{1,0:T(8,128)} fusion(f32[1024,2048]{1,0:T(8,128)S(1)} %bitcast.7, f32[1024,2048]{1,0:T(8,128)S(1)} %bitcast.6), kind=kOutput, calls=%fused_computation.21 | convolution fusion | flops 25769803776 | bytes 20971520 | tf_op jit(solution)/shard_map/dot_general | solution.py:15
  138.0 0.0 copy-start
  138.0 0.0 reduce-scatter.2.cloned.1.call-update
  138.0 4.0 %multiply_reduce_fusion = f32[1024]{0:T(1024)S(1)} fusion(f32[1024,2048]{1,0:T(8,128)} %param.5), kind=kLoop, calls=%fused_computation.1 | loop fusion | flops 4193280 | bytes 8392704 | tf_op jit(solution)/shard_map/reduce_sum | solution.py:40
  142.0 35.9 %all-gather = f32[16384]{0:T(1024)S(1)} all-gather(f32[1024]{0:T(1024)S(1)} %multiply_reduce_fusion), channel_id=2, replica_groups=mesh['ex'=16,'co'=16] {'co'}, dimensions={0}, use_global_device_ids=true | all-gather | bytes 69632 | tf_op jit(solution)/shard_map/all_gather | solution.py:11
  177.9 0.0 copy-done
  177.9 42.4 %reduce-scatter.2.cloned.1.call-done = f32[64,1024]{1,0:T(8,128)} async-done(((f32[1024,1024]{1,0:T(8,128)}), f32[64,1024]{1,0:T(8,128)}) %reduce-scatter.2.cloned.1.call-update) | async-done | bytes 262160 | tf_op jit(solution)/shard_map/reduce_scatter | solution.py:45
  220.4 1.0 multiply_bitcast_fusion
  221.3 0.2 copy.10
  221.5 3.2 %scatter_custom_fusion = f32[64,1024]{0,1:T(8,128)S(1)} fusion(s32[1024]{0:T(1024)S(1)} %compare_select_fusion, f32[1024,64]{1,0:T(8,128)S(1)} %copy.10, f32[]{:T(128)} %constant.11.clone.1), kind=kCustom, calls=%fused_computation.4 | custom fusion | bytes 262148 | tf_op jit(solution)/shard_map/scatter | solution.py:50
  224.8 0.9 copy.11
  (6 shorter events, 0.1 us)
Async XLA Ops:
  6.5 213.8 %reduce-scatter.2.cloned.1.call-start = ((), (), s32[]{:S(2)}) async-start(), calls=%async_computation.2 | async-start | bytes 4456448 | tf_op jit(solution)/shard_map/reduce_scatter | solution.py:45
  8.6 101.6 %slice-start = ((s8[8388608]{0:T(1024)(128)(4,1)}), s8[4194304]{0:T(1024)(128)(4,1)S(1)}, s32[]{:S(2)}) async-start(s8[8388608]{0:T(1024)(128)(4,1)} %bitcast.5), calls=%async_computation.3 | async-start | bytes 8388608
  9.7 100.6 %slice-start.1 = ((s8[8388608]{0:T(1024)(128)(4,1)}), s8[4194304]{0:T(1024)(128)(4,1)S(1)}, s32[]{:S(2)}) async-start(s8[8388608]{0:T(1024)(128)(4,1)} %bitcast.5), calls=%async_computation.4 | async-start | bytes 8388608
  138.0 39.9 %copy-start = (s32[1024]{0:T(1024)S(1)}, s32[1024]{0:T(1024)}, u32[]{:S(2)}) copy-start(s32[1024]{0:T(1024)} %param.9) | copy-start | bytes 12292
Sparse Core Ops, SparseCore 0:
  138.1 82.1 reduce-scatter.1
